TPU v7x, 32 devices: a whole 2x2x4 slice. The times are simulated.
32 devices in a mesh: req: 8 (over z, x), tp: 4 (over y, core).
Axes of the slice: x: 2, y: 2, z: 4, core: 2. Of those that a mesh axis runs over, the one named last changes fastest.
Arguments:
- tokens: bfloat16 [4096, 3584], P('req'), may hold values from -400 to 400, as said below
- norm_gain: float32 [3584], P(('req', 'tp')), may hold values from 0.5 to 1.5
- qkv_weight: float32 [3584, 4608], P(('req', 'tp')), may hold values from -0.09375 to 0.09375
- qkv_bias: float32 [4608], P(('req', 'tp')), may hold values from -48 to 48
- lengths: int32 [8, 4], P('req'), may hold values from 1 to 256, 512 in all within a row
Outputs:
- context: bfloat16 [4096, 3584], P('req', 'tp')
Inputs may be any that keep to these rules, and one draw needn't show every extreme that they name: `tokens`: hidden states of order one to some hundreds. Each replica's tenant lengths sum to 512, the largest is exactly 256.
All inputs are finite; a program needn't handle non-finite values.
Results may differ from a plain program's by a relative error of at most 0.009.
The roundings to bfloat16 on the way count: a program that leaves them out, or rounds other values in their place, can miss the bound.
Values may be sent and summed in bfloat16 or wider, within the bound.
A program may use at most 128 MiB of HBM per device.

v0:
```python
import math

import jax
import jax.numpy as jnp
from jax import lax
from jax.sharding import PartitionSpec as P

HEAD_DIM = 128
SINKS = 4
GROUP = 7
WINDOW = 160


def normalize(values, gain):
    wide = values.astype(jnp.float32)
    meansq = jnp.mean(wide * wide, axis=-1, keepdims=True)
    return (wide * lax.rsqrt(meansq + 1e-06) * gain.astype(jnp.float32)).astype(jnp.bfloat16)


def positions(lens, count):
    index = jnp.arange(count, dtype=jnp.int32)
    ends = jnp.cumsum(lens)
    after = index[:, None] >= ends[None, :]
    tenant = jnp.sum(after.astype(jnp.int32), axis=1)
    start = jnp.sum(jnp.where(after, lens[None, :], 0), axis=1)
    return (tenant, index - start)


def rotate(values, pos):
    half = HEAD_DIM // 2
    freqs = jnp.exp(-(jnp.arange(half, dtype=jnp.float32) * 2.0 / HEAD_DIM) * math.log(1000000.0))
    angle = pos.astype(jnp.float32)[:, None] * freqs[None, :]
    cosine = jnp.concatenate([jnp.cos(angle), jnp.cos(angle)], axis=-1)
    sine = jnp.concatenate([jnp.sin(angle), jnp.sin(angle)], axis=-1)
    shape = (values.shape[0],) + (1,) * (values.ndim - 2) + (HEAD_DIM,)
    cosine = cosine.reshape(shape)
    sine = sine.reshape(shape)
    turned = jnp.concatenate([-values[..., half:], values[..., :half]], axis=-1)
    return values * cosine + turned * sine


def attend(joined, tenant, pos):
    count = joined.shape[0]
    blocks = joined.reshape(count, -1, GROUP + 2, HEAD_DIM)
    query = rotate(blocks[:, :, :GROUP], pos).astype(jnp.bfloat16)
    key_part = rotate(blocks[:, :, GROUP], pos).astype(jnp.bfloat16)
    value_part = blocks[:, :, GROUP + 1].astype(jnp.bfloat16)
    scores = jnp.einsum(
        "qghd,kgd->ghqk", query, key_part, preferred_element_type=jnp.float32
    ) / math.sqrt(HEAD_DIM)
    same = tenant[:, None] == tenant[None, :]
    causal = pos[None, :] <= pos[:, None]
    near = jnp.logical_or(pos[:, None] - pos[None, :] < WINDOW, pos[None, :] < SINKS)
    allowed = jnp.logical_and(jnp.logical_and(same, causal), near)
    scores = jnp.where(allowed[None, None], scores, -1e30)
    peak = jnp.max(scores, axis=-1, keepdims=True)
    expo = jnp.where(allowed[None, None], jnp.exp(scores - peak), 0.0)
    weights = (expo / jnp.sum(expo, axis=-1, keepdims=True)).astype(jnp.bfloat16)
    mixed = jnp.einsum("ghqk,kgd->qghd", weights, value_part, preferred_element_type=jnp.float32)
    return mixed.reshape(count, -1).astype(jnp.bfloat16)


def shards(tokens, norm_gain, qkv_weight, qkv_bias, lengths):
    tp_count = lax.axis_size("tp")
    req_count = lax.axis_size("req")
    tp_place = lax.axis_index("tp")
    gain_full, bias_full = (
        lax.all_gather(norm_gain.astype(jnp.bfloat16), ("req", "tp"), axis=0, tiled=True),
        lax.all_gather(qkv_bias.astype(jnp.bfloat16), ("req", "tp"), axis=0, tiled=True),
    )
    width = bias_full.shape[0] // tp_count
    bias_block = lax.dynamic_slice_in_dim(bias_full, tp_place * width, width).astype(jnp.float32)
    normed = normalize(tokens, gain_full)
    weight_b = qkv_weight.astype(jnp.bfloat16)
    count = tokens.shape[0]
    gathered = lax.all_gather(weight_b, "req", axis=0, tiled=True)
    regrouped = lax.all_to_all(gathered, "tp", split_axis=1, concat_axis=0, tiled=True)
    shard_rows = weight_b.shape[0]
    reordered = (
        normed.reshape(count, req_count, tp_count, shard_rows)
        .transpose(0, 2, 1, 3)
        .reshape(count, -1)
    )
    joined = jnp.dot(reordered, regrouped, preferred_element_type=jnp.float32)
    joined = joined + bias_block[None, :]
    tenant, pos = positions(lengths[0], count)
    return attend(joined, tenant, pos)


def solution(mesh):
    placed = (
        P("req", None),
        P(("req", "tp")),
        P(("req", "tp"), None),
        P(("req", "tp")),
        P("req", None),
    )
    return jax.shard_map(
        shards, mesh=mesh, in_specs=placed, out_specs=P("req", "tp"), check_vma=False
    )
```

profile of v0, /device:TPU:0, one launch (start us, length us, event | category | flops | bytes accessed | tf_op | source)
XLA Modules:
  0.0 330.9 jit_solution(9403856503985649453)
XLA Ops:
  6.5 0.0 all-gather.2.cloned.1.call-start
  6.5 2.7 convert_element_type.70
  9.3 0.0 all-gather.2.cloned.1.call-update
  9.3 126.2 %all-gather.2.cloned.1.call-done = bf16[896,4608]{1,0:T(8,128)(2,1)} async-done(((bf16[112,4608]{1,0:T(8,128)(2,1)}), bf16[896,4608]{1,0:T(8,128)(2,1)}) %all-gather.2.cloned.1.call-update) | async-done | bytes 8257552 | tf_op jit(solution)/shard_map/all_gather | solution.py:76
  135.5 11.4 %copy.40 = bf16[896,4608]{0,1:T(8,128)(2,1)} copy(bf16[896,4608]{1,0:T(8,128)(2,1)} %all-gather.2.cloned.1.call-done) | data formatting | bytes 16515072 | tf_op jit(solution)/shard_map/all_gather | solution.py:76
  146.9 5.8 %all-to-all-start = ((bf16[896,4,1152]{0,2,1:T(8,128)(2,1)}), bf16[896,4,1152]{0,2,1:T(8,128)(2,1)}, u32[]{:S(2)}, u32[]{:S(2)}) async-start(bf16[896,4,1152]{0,2,1:T(8,128)(2,1)} %bitcast.65), calls=%async_computation | async-start | bytes 16515072 | tf_op jit(solution)/shard_map/all_to_all | solution.py:77
  152.7 0.0 copy-done.2
  152.7 0.0 copy-done.1
  152.7 0.0 copy-done
  152.7 0.2 reduce-window.8
  152.9 0.2 dynamic-update-slice
  153.1 0.2 dynamic-update-slice.1
  153.3 122.7 %all-reduce.2 = (bf16[3584]{0:T(1024)(128)(2,1)S(1)}, bf16[4608]{0:T(1024)(128)(2,1)S(1)}) all-reduce(bf16[3584]{0:T(1024)(128)(2,1)S(1)} %dynamic-update-slice, bf16[4608]{0:T(1024)(128)(2,1)S(1)} %dynamic-update-slice.1), channel_id=1, replica_groups=mesh['req'=8,'tp'=4] {'req','tp'}, use_global_device_ids=true, to_apply=%add | all-reduce | flops 8192 | bytes 32768
  276.0 5.9 %copy.38 = bf16[512,3584]{0,1:T(8,128)(2,1)} copy(bf16[512,3584]{1,0:T(8,128)(2,1)} %param.5) | data formatting | bytes 7340032 | tf_op args[0]
  282.0 2.9 fusion
  284.9 3.1 fusion.2
  288.0 2.0 copy.39
  290.0 0.1 dynamic-slice_convert_fusion
  290.1 0.1 convert_reduce_fusion
  290.2 0.5 fusion.27
  290.7 0.1 pad_maximum_fusion
  290.8 0.5 multiply_cosine_fusion.1
  291.3 0.4 fusion.14
  291.8 0.0 all-to-all-done
  291.8 11.5 %copy.41 = bf16[4,896,1152]{2,1,0:T(8,128)(2,1)} copy(bf16[4,896,1152]{1,2,0:T(8,128)(2,1)} %bitcast.4) | data formatting | bytes 16515072 | tf_op jit(solution)/shard_map/all_to_all | solution.py:77
  303.3 10.8 %convolution_add_fusion = f32[512,1152]{1,0:T(8,128)} fusion(bf16[512,3584]{0,1:T(8,128)(2,1)} %bitcast.72, bf16[3584,1152]{1,0:T(8,128)(2,1)} %bitcast.71, f32[1152]{0:T(1024)S(1)} %dynamic-slice_convert_fusion), kind=kOutput, calls=%fused_computation.13 | convolution fusion | flops 4228448256 | bytes 14291456 | tf_op jit(solution)/shard_map/dot_general | solution.py:84
  314.1 2.2 copy.42
  316.4 0.2 slice_negate_fusion
  316.6 1.7 fusion.3
  318.3 1.8 fusion.4
  320.1 2.7 fusion.10
  322.7 1.3 copy.46
  (14 shorter events, 0.1 us)
Async XLA Ops:
  6.5 128.9 %all-gather.2.cloned.1.call-start = ((), (), s32[]{:S(2)}) async-start(), calls=%async_computation.1 | async-start | bytes 9289728 | tf_op jit(solution)/shard_map/all_gather | solution.py:76
  146.9 5.8 %copy-start.2 = (f32[112]{0:T(128)S(1)}, f32[112]{0:T(128)}, u32[]{:S(2)}) copy-start(f32[112]{0:T(128)} %param.6) | copy-start | bytes 1348
  146.9 5.8 %copy-start.1 = (f32[144]{0:T(256)S(1)}, f32[144]{0:T(256)}, u32[]{:S(2)}) copy-start(f32[144]{0:T(256)} %param.8) | copy-start | bytes 1732
  146.9 5.8 %copy-start = (s32[1,4]{1,0:T(1,128)S(1)}, s32[1,4]{1,0:T(1,128)}, u32[]{:S(2)}) copy-start(s32[1,4]{1,0:T(1,128)} %param.9) | copy-start | bytes 52
  146.9 144.8 %all-to-all-start = ((bf16[896,4,1152]{0,2,1:T(8,128)(2,1)}), bf16[896,4,1152]{0,2,1:T(8,128)(2,1)}, u32[]{:S(2)}, u32[]{:S(2)}) async-start(bf16[896,4,1152]{0,2,1:T(8,128)(2,1)} %bitcast.65), calls=%async_computation | async-start | bytes 16515072 | tf_op jit(solution)/shard_map/all_to_all | solution.py:77
Sparse Core Ops, SparseCore 0:
  9.5 125.8 all-gather.1
where the time goes:
time: 332 us; the launch traced here: 331 us
  waiting for transfers between devices  126 us (38%)
  blocking collectives  123 us (37%)
  local copies, waits for them, and re-layouts  34.9 us (11%)
  matrix products  15.2 us (5%)
  between operations  13.6 us (4%)
  other arithmetic  12.6 us (4%)
  starting transfers between devices  5.76 us (2%)
    all_gather x1, waiting for transfers between devices, shards(): gathered = lax.all_gather(weight_b, 'req', axis=0, tiled=True)  126 us
    unnamed x1, blocking collectives  123 us
    all_to_all x1, local copies, waits for them, and re-layouts, shards(): lax.all_to_all(gathered, 'tp', split_axis=1, concat_axis=0, tiled=True)  11.5 us
    all_gather x1, local copies, waits for them, and re-layouts, shards(): gathered = lax.all_gather(weight_b, 'req', axis=0, tiled=True)  11.4 us
    dot_general x1, matrix products, shards(): joined = jnp.dot(reordered, regrouped, preferred_element_type=jnp.float32)  10.8 us
  transfers between devices with their start and end apart: 2, of which 1 were waited for; matrix products, arithmetic and copies ran while one was open for 5% of the time, Pallas kernels for 0%

commit v1 on v0

v1 whole, which is shorter than its diff:
```python
import functools
import math

import jax
import jax.numpy as jnp
from jax import lax
from jax.experimental import pallas as pl
from jax.experimental.pallas import tpu as pltpu
from jax.sharding import PartitionSpec as P

HEAD_DIM = 128
SINKS = 4
GROUP = 7
WINDOW = 160
MOST = 256
MESH = pl.DeviceIdType.MESH


def normalize(values, gain):
    wide = values.astype(jnp.float32)
    meansq = jnp.mean(wide * wide, axis=-1, keepdims=True)
    return (wide * lax.rsqrt(meansq + 1e-06) * gain.astype(jnp.float32)).astype(jnp.bfloat16)


def starts(lens, count):
    index = jnp.arange(count, dtype=jnp.int32)
    after = index[:, None] >= jnp.cumsum(lens)[None, :]
    return jnp.sum(jnp.where(after, lens[None, :], 0), axis=1)


def tables(lens, count):
    half = HEAD_DIM // 2
    pos = jnp.arange(count, dtype=jnp.int32) - starts(lens, count)
    freqs = jnp.exp(-(jnp.arange(half, dtype=jnp.float32) * 2.0 / HEAD_DIM) * math.log(1000000.0))
    angle = pos.astype(jnp.float32)[:, None] * freqs[None, :]
    cosine, sine = jnp.cos(angle), jnp.sin(angle)
    return (
        jnp.concatenate([cosine, cosine], axis=-1),
        jnp.concatenate([-sine, sine], axis=-1),
    )


def attend_kernel(lens_ref, joined_ref, cos_ref, sin_ref, out_ref):
    count = joined_ref.shape[0]
    tenants = lens_ref.shape[1]
    block = 128

    def turned(lo, size, column):
        v = joined_ref[lo : lo + size, column * HEAD_DIM : (column + 1) * HEAD_DIM]
        r = v * cos_ref[lo : lo + size, :] + pltpu.roll(v, HEAD_DIM // 2, 1) * sin_ref[lo : lo + size, :]
        return r.astype(jnp.bfloat16)

    keys = [turned(lo, block, GROUP) for lo in range(0, count, block)]
    values = joined_ref[:, (GROUP + 1) * HEAD_DIM :].astype(jnp.bfloat16)
    back = -(-(MOST - 1) // block)
    for at in range(count // block):
        first = max(0, at - back)
        wide = (at + 1 - first) * block
        query_at = at * block + lax.broadcasted_iota(jnp.int32, (block, 1), 0)
        key_at = first * block + lax.broadcasted_iota(jnp.int32, (block, wide), 1)
        start = jnp.zeros((block, 1), jnp.int32)
        end = jnp.int32(0)
        for t in range(tenants):
            end = end + lens_ref[0, t]
            start = jnp.where(query_at >= end, end, start)
        low = jnp.maximum(query_at - (WINDOW - 1), start)
        allowed = jnp.logical_and(
            key_at <= query_at,
            jnp.logical_or(
                key_at >= low, jnp.logical_and(key_at >= start, key_at < start + SINKS)
            ),
        )
        key_block = jnp.concatenate(keys[first : at + 1], axis=0)
        value_block = values[first * block : (at + 1) * block]
        for head in range(GROUP):
            query = turned(at * block, block, head)
            scores = lax.dot_general(
                query, key_block, (((1,), (1,)), ((), ())), preferred_element_type=jnp.float32
            ) * (1.0 / math.sqrt(HEAD_DIM))
            scores = jnp.where(allowed, scores, -1e30)
            peak = jnp.max(scores, axis=-1, keepdims=True)
            expo = jnp.exp(scores - peak)
            weights = (expo * (1.0 / jnp.sum(expo, axis=-1, keepdims=True))).astype(jnp.bfloat16)
            mixed = jnp.dot(weights, value_block, preferred_element_type=jnp.float32)
            out_ref[at * block : (at + 1) * block, head * HEAD_DIM : (head + 1) * HEAD_DIM] = (
                mixed.astype(jnp.bfloat16)
            )


def attend(joined, lens):
    count = joined.shape[0]
    cosine, sine = tables(lens[0], count)
    vmem = pl.BlockSpec(memory_space=pltpu.VMEM)
    return pl.pallas_call(
        attend_kernel,
        out_shape=jax.ShapeDtypeStruct((count, GROUP * HEAD_DIM), jnp.bfloat16),
        in_specs=[pl.BlockSpec(memory_space=pltpu.SMEM), vmem, vmem, vmem],
        out_specs=vmem,
        compiler_params=pltpu.CompilerParams(vmem_limit_bytes=32 << 20),
        name="attention",
    )(lens, joined, cosine, sine)


def project_kernel(
    w_ref, side_ref, tok_hbm, out_ref,
    wb, full, tok, normed, scale, sides, tok_sem,
    first_send, first_recv, side_send, side_recv,
    ring_send, ring_recv, trail_send, trail_recv,
):
    req, tp = lax.axis_index("req"), lax.axis_index("tp")
    count, depth = tok.shape
    shard, width = full.shape[1:]
    z, x = req // 2, req % 2
    y, core = tp // 2, tp % 2
    place = (1 - x) * z + x * (7 - z)

    def req_at(pos):
        pos = pos % 8
        far = pos // 4
        return (1 - far) * (2 * pos) + far * (2 * (7 - pos) + 1)

    right, left = req_at(place + 1), req_at(place + 7)
    peers = (2 * y + 1 - core, 2 * (1 - y) + core, 2 * (1 - y) + 1 - core)
    own = 4 * req + tp

    tok_copy = pltpu.make_async_copy(tok_hbm, tok, tok_sem)
    tok_copy.start()

    barrier = pltpu.get_barrier_semaphore()
    for peer in peers:
        pl.semaphore_signal(barrier, inc=1, device_id=(req, peer), device_id_type=MESH)
    for near in (left, right):
        pl.semaphore_signal(barrier, inc=1, device_id=(near, tp), device_id_type=MESH)

    def columns(t):
        return w_ref[:, pl.ds(pl.multiple_of(t * width, 128), width)].astype(jnp.bfloat16)

    wb[0] = columns(peers[0])
    full[own] = columns(tp)
    sides[own] = side_ref[...]
    pl.semaphore_wait(barrier, 5)

    firsts, side_firsts = [], []
    for k, peer in enumerate(peers):
        if k:
            wb[k] = columns(peer)
        copy = pltpu.make_async_remote_copy(
            src_ref=wb.at[k], dst_ref=full.at[own],
            send_sem=first_send.at[k], recv_sem=first_recv.at[k],
            device_id=(req, peer), device_id_type=MESH,
        )
        copy.start()
        firsts.append(copy)
    for k, peer in enumerate(peers):
        copy = pltpu.make_async_remote_copy(
            src_ref=side_ref, dst_ref=sides.at[own],
            send_sem=side_send.at[k], recv_sem=side_recv.at[k],
            device_id=(req, peer), device_id_type=MESH,
        )
        copy.start()
        side_firsts.append(copy)

    ring = {}
    trail = {}

    def send(way, hop, piece):
        source = req_at(place + 8 - hop) if way == 0 else req_at(place + hop)
        row = y if piece == 0 else 1 - y
        slot = 4 * source + 2 * row + way
        copy = pltpu.make_async_remote_copy(
            src_ref=full.at[slot], dst_ref=full.at[slot],
            send_sem=ring_send.at[way, hop, piece], recv_sem=ring_recv.at[way, hop, piece],
            device_id=(right if way == 0 else left, tp), device_id_type=MESH,
        )
        copy.start()
        ring[way, hop, piece] = copy

    def send_trail(hop):
        rows = pl.ds(4 * req_at(place + 8 - hop), 4)
        copy = pltpu.make_async_remote_copy(
            src_ref=sides.at[rows], dst_ref=sides.at[rows],
            send_sem=trail_send.at[hop], recv_sem=trail_recv.at[hop],
            device_id=(right, tp), device_id_type=MESH,
        )
        copy.start()
        trail[hop] = copy

    def spread(row, parts, step):
        total = step * len(parts)
        line = jnp.zeros((8, total), jnp.float32)
        for i, part in enumerate(parts):
            have = part.shape[1]
            padded = jnp.concatenate([part, jnp.zeros((8, total - have), jnp.float32)], axis=1)
            line = line + (pltpu.roll(padded, step * i, 1) if i else padded)
        return line[row : row + 1, :]

    group = depth // 4

    def chunk(c, begin, bias):
        gain = spread(0, [sides[8 * c + i] for i in range(8)], shard)
        offset = pl.multiple_of(c * group, 128)

        @pl.loop(0, count // 64)
        def _(i):
            rows = pl.ds(pl.multiple_of(i * 64, 64), 64)
            wide = tok[rows, pl.ds(offset, group)].astype(jnp.float32)
            normed[rows, :] = (wide * scale[rows, :][:, :1] * gain).astype(jnp.bfloat16)

        for n in range(3):
            part = width // 3
            lo = n * part
            block = full[pl.ds(8 * c, 8), :, lo : lo + part].reshape(group, part)
            product = jnp.dot(normed[...], block, preferred_element_type=jnp.float32)
            if begin:
                out_ref[:, lo : lo + part] = product
            elif bias is None:
                out_ref[:, lo : lo + part] += product
            else:
                out_ref[:, lo : lo + part] += product + bias[:, lo : lo + part]

    inner = (z % 3 + 2) // 3
    order0 = inner * z + (1 - inner) * (3 - z)
    order1 = (z + 2) % 4
    order2 = (z * 3) // 4
    order3 = 6 - order0 - order1 - order2

    for step in range(8):
        for way in range(2):
            if step == 0 and way == 0:
                firsts[0].wait_recv()
            if step >= 1:
                ring[way, step - 1, 0].wait_recv()
            if step <= 6:
                send(way, step, 0)
        if step >= 1:
            for way in range(2):
                if step == 1 and way == 0:
                    firsts[1].wait_recv()
                    firsts[2].wait_recv()
                if step >= 2:
                    ring[way, step - 2, 1].wait_recv()
                send(way, step - 1, 1)
            if step == 1:
                for copy in side_firsts:
                    copy.wait_recv()
            else:
                trail[step - 2].wait_recv()
            send_trail(step - 1)
        if step == 0:
            tok_copy.wait()

            @pl.loop(0, count // 32)
            def _(i):
                rows = pl.ds(pl.multiple_of(i * 32, 32), 32)
                wide = tok[rows, :].astype(jnp.float32)
                mean = jnp.sum(wide * wide, axis=-1, keepdims=True) * (1.0 / depth)
                scale[rows, :] = jnp.broadcast_to(lax.rsqrt(mean + 1e-06), (32, 128))
        elif step == 6:
            chunk(order0, True, None)
        elif step == 7:
            chunk(order1, False, None)
    for way in range(2):
        ring[way, 6, 1].wait_recv()
    trail[6].wait_recv()
    bias = spread_bias(sides, tp, width)
    chunk(order2, False, None)
    chunk(order3, False, bias)
    for copy in firsts + side_firsts + list(ring.values()) + list(trail.values()):
        copy.wait_send()


def spread_bias(sides, tp, width):
    step = width // 8
    line = jnp.zeros((8, width), jnp.float32)
    for i in range(8):
        both = sides[8 * tp + i]
        head = pltpu.roll(both, 7, 0)
        tail = pltpu.roll(both, 6, 0)
        padded = jnp.concatenate([head, tail, jnp.zeros((8, width - 256), jnp.float32)], axis=1)
        line = line + (pltpu.roll(padded, step * i, 1) if i else padded)
    return line[0:1, :]


def project(tokens, norm_gain, qkv_weight, qkv_bias):
    count, depth = tokens.shape
    shard, total = qkv_weight.shape
    width = total // 4
    line = lambda v, size: jnp.pad(v.astype(jnp.bfloat16).astype(jnp.float32), (0, size - v.shape[0]))
    side = jnp.concatenate([line(norm_gain, 128), line(qkv_bias, 896)]).reshape(8, 128)
    vmem = pl.BlockSpec(memory_space=pltpu.VMEM)
    dma = pltpu.SemaphoreType.DMA
    return pl.pallas_call(
        project_kernel,
        out_shape=jax.ShapeDtypeStruct((count, width), jnp.float32),
        in_specs=[vmem, vmem, pl.BlockSpec(memory_space=pl.ANY)],
        out_specs=vmem,
        scratch_shapes=[
            pltpu.VMEM((3, shard, width), jnp.bfloat16),
            pltpu.VMEM((32, shard, width), jnp.bfloat16),
            pltpu.VMEM((count, depth), jnp.bfloat16),
            pltpu.VMEM((count, depth // 4), jnp.bfloat16),
            pltpu.VMEM((count, 128), jnp.float32),
            pltpu.VMEM((32, 8, 128), jnp.float32),
            dma,
            dma((3,)), dma((3,)), dma((3,)), dma((3,)),
            dma((2, 7, 2)), dma((2, 7, 2)), dma((7,)), dma((7,)),
        ],
        compiler_params=pltpu.CompilerParams(
            collective_id=0, has_side_effects=True, vmem_limit_bytes=48 << 20
        ),
        name="project",
    )(qkv_weight, side, tokens)


def project_plain(tokens, norm_gain, qkv_weight, qkv_bias):
    tp_count = lax.axis_size("tp")
    req_count = lax.axis_size("req")
    tp_place = lax.axis_index("tp")
    gain_full, bias_full = (
        lax.all_gather(norm_gain.astype(jnp.bfloat16), ("req", "tp"), axis=0, tiled=True),
        lax.all_gather(qkv_bias.astype(jnp.bfloat16), ("req", "tp"), axis=0, tiled=True),
    )
    width = bias_full.shape[0] // tp_count
    bias_block = lax.dynamic_slice_in_dim(bias_full, tp_place * width, width).astype(jnp.float32)
    normed = normalize(tokens, gain_full)
    weight_b = qkv_weight.astype(jnp.bfloat16)
    count = tokens.shape[0]
    gathered = lax.all_gather(weight_b, "req", axis=0, tiled=True)
    regrouped = lax.all_to_all(gathered, "tp", split_axis=1, concat_axis=0, tiled=True)
    shard_rows = weight_b.shape[0]
    reordered = (
        normed.reshape(count, req_count, tp_count, shard_rows)
        .transpose(0, 2, 1, 3)
        .reshape(count, -1)
    )
    joined = jnp.dot(reordered, regrouped, preferred_element_type=jnp.float32)
    return joined + bias_block[None, :]


def shards(small, tokens, norm_gain, qkv_weight, qkv_bias, lengths):
    form = project if small else project_plain
    return attend(form(tokens, norm_gain, qkv_weight, qkv_bias), lengths)


def solution(mesh):
    placed = (
        P("req", None),
        P(("req", "tp")),
        P(("req", "tp"), None),
        P(("req", "tp")),
        P("req", None),
    )
    small = mesh.shape["req"] == 8 and mesh.shape["tp"] == 4
    return jax.shard_map(
        functools.partial(shards, small),
        mesh=mesh, in_specs=placed, out_specs=P("req", "tp"), check_vma=False,
    )
```

time: 332 us -> 111 us (0.33)
  waiting for transfers between devices: 126 us -> 0 us
  blocking collectives: 123 us -> 0 us
  Pallas kernels: 0 us -> 106 us
  local copies, waits for them, and re-layouts: 34.9 us -> 0.01 us
  matrix products: 15.2 us -> 0 us
  between operations: 13.6 us -> 0.05 us
  other arithmetic: 12.6 us -> 4.27 us
  starting transfers between devices: 5.76 us -> 0 us
    all_gather x1 -> x0, waiting for transfers between devices: 126 us -> none  [shards(): gathered = lax.all_gather(weight_b, 'req', axis=0, tiled=True)]
    unnamed x1 -> x0, blocking collectives: 123 us -> none
    pallas_call x0 -> x2, Pallas kernels: none -> 106 us  [the longest x1 96.4 us: project(): pl.pallas_call(project_kernel, out_shape=jax.ShapeDtypeStruct((count, wid...]
    dot_general x3 -> x0, matrix products: 15.2 us -> none  [the longest x1 10.8 us: shards(): joined = jnp.dot(reordered, regrouped, preferred_element_type=jnp.float32)]
    all_to_all x1 -> x0, local copies, waits for them, and re-layouts: 11.5 us -> none  [shards(): lax.all_to_all(gathered, 'tp', split_axis=1, concat_axis=0, tiled=True)]
    all_gather x1 -> x0, local copies, waits for them, and re-layouts: 11.4 us -> none  [shards(): gathered = lax.all_gather(weight_b, 'req', axis=0, tiled=True)]
    unnamed x11 -> x4, local copies, waits for them, and re-layouts: 6.38 us -> 0.01 us
    all_to_all x1 -> x0, starting transfers between devices: 5.76 us -> none  [shards(): lax.all_to_all(gathered, 'tp', split_axis=1, concat_axis=0, tiled=True)]
  transfers between devices with their start and end apart: 2 -> 0, of which waited for: 1 -> 0; matrix products, arithmetic and copies ran while one was open for 5% -> 0% of each run, Pallas kernels for 0% -> 0%
where the time goes in v1:
time: 111 us
  Pallas kernels  106 us (95%)
  other arithmetic  4.27 us (4%)
    pallas_call x1, Pallas kernels, project(): pl.pallas_call(project_kernel, out_shape=jax.ShapeDtypeStruct((count, wid...  96.4 us
    pallas_call x1, Pallas kernels, attend(): pl.pallas_call(attend_kernel, out_shape=jax.ShapeDtypeStruct((count, GROU...  10.1 us

profile of v1, /device:TPU:0, one launch (start us, length us, event | category | flops | bytes accessed | tf_op | source)
XLA Modules:
  0.0 110.8 jit_solution(6122568548317156787)
XLA Ops:
  0.0 0.0 copy-start
  0.0 0.8 convert_element_type.19
  0.8 0.7 convert_element_type.20
  1.5 0.8 reduce-window.8
  2.3 0.7 select_reduce_fusion
  3.1 1.0 fusion
  4.1 0.2 pad_maximum_fusion
  4.3 0.0 copy-done
  4.3 0.0 copy-start.1
  4.3 96.4 %project.1.joined_ref = f32[512,1152]{1,0:T(8,128)S(1)} custom-call(f32[112,4608]{1,0:T(8,128)S(1)} %copy-done, f32[8,128]{1,0:T(8,128)S(1)} %fusion.5.side_ref, bf16[512,3584]{1,0:T(8,128)(2,1)} %tok_hbm.1), custom_call_target="tpu_custom_call" | custom-call | tf_op jit(solution)/shard_map/project/pallas_call | solution.py:292
  100.7 0.0 copy-done.1
  100.7 10.1 %attention.1 = bf16[512,896]{1,0:T(8,128)(2,1)} custom-call(s32[1,4]{1,0:T(1,128)S(1)} %copy-done.1, f32[512,1152]{1,0:T(8,128)S(1)} %project.1.joined_ref, f32[512,128]{1,0:T(8,128)S(1)} %get-tuple-element.8.cos_ref, f32[512,128]{1,0:T(8,128)S(1)} %get-tuple-element.9.sin_ref), custom_call_target="tpu_custom_call" | custom-call | tf_op jit(solution)/shard_map/attention/pallas_call | solution.py:94
  (3 shorter events, 0.0 us)
Async XLA Ops:
  0.0 4.3 %copy-start = (f32[112,4608]{1,0:T(8,128)S(1)}, f32[112,4608]{1,0:T(8,128)}, u32[]{:S(2)}) copy-start(f32[112,4608]{1,0:T(8,128)} %w_ref.1) | copy-start | bytes 6193156
  4.3 96.4 %copy-start.1 = (s32[1,4]{1,0:T(1,128)S(1)}, s32[1,4]{1,0:T(1,128)}, u32[]{:S(2)}) copy-start(s32[1,4]{1,0:T(1,128)} %lens_ref.1) | copy-start | bytes 52

commit v2 on v0

v2 whole, which is shorter than its diff:
```python
import functools
import math

import jax
import jax.numpy as jnp
from jax import lax
from jax.experimental import pallas as pl
from jax.experimental.pallas import tpu as pltpu
from jax.sharding import PartitionSpec as P

HEAD_DIM = 128
SINKS = 4
GROUP = 7
WINDOW = 160
MOST = 256
MESH = pl.DeviceIdType.MESH


def normalize(values, gain):
    wide = values.astype(jnp.float32)
    meansq = jnp.mean(wide * wide, axis=-1, keepdims=True)
    return (wide * lax.rsqrt(meansq + 1e-06) * gain.astype(jnp.float32)).astype(jnp.bfloat16)


def starts(lens, count):
    index = jnp.arange(count, dtype=jnp.int32)
    after = index[:, None] >= jnp.cumsum(lens)[None, :]
    return jnp.sum(jnp.where(after, lens[None, :], 0), axis=1)


def rotated(v, cosine, sine):
    return (v * cosine + pltpu.roll(v, HEAD_DIM // 2, 1) * sine).astype(jnp.bfloat16)


def start_of(query_at, lens_ref):
    start, end = jnp.zeros_like(query_at), jnp.int32(0)
    for t in range(lens_ref.shape[1]):
        end = end + lens_ref[0, t]
        start = jnp.where(query_at >= end, end, start)
    return start


def attend_kernel(lens_ref, qkv_ref, out_ref):
    count = qkv_ref.shape[0]
    block = 128
    back = -(-(MOST - 1) // block)
    for at in range(count // block):
        first = max(0, at - back)
        wide = (at + 1 - first) * block
        rows = slice(at * block, (at + 1) * block)
        seen = slice(first * block, (at + 1) * block)
        query_at = at * block + lax.broadcasted_iota(jnp.int32, (block, 1), 0)
        key_at = first * block + lax.broadcasted_iota(jnp.int32, (block, wide), 1)
        start = start_of(query_at, lens_ref)
        low = jnp.maximum(query_at - (WINDOW - 1), start)
        allowed = jnp.logical_and(
            key_at <= query_at,
            jnp.logical_or(
                key_at >= low, jnp.logical_and(key_at >= start, key_at < start + SINKS)
            ),
        )
        query = jnp.concatenate(
            [qkv_ref[rows, h * HEAD_DIM : (h + 1) * HEAD_DIM] for h in range(GROUP)], axis=0
        )
        scores = lax.dot_general(
            query, qkv_ref[seen, GROUP * HEAD_DIM : (GROUP + 1) * HEAD_DIM],
            (((1,), (1,)), ((), ())), preferred_element_type=jnp.float32,
        ) * (1.0 / math.sqrt(HEAD_DIM))
        scores = jnp.where(allowed[None], scores.reshape(GROUP, block, wide), -1e30)
        peak = jnp.max(scores, axis=-1, keepdims=True)
        expo = jnp.exp(scores - peak)
        weights = (expo * (1.0 / jnp.sum(expo, axis=-1, keepdims=True))).astype(jnp.bfloat16)
        mixed = jnp.dot(
            weights.reshape(GROUP * block, wide), qkv_ref[seen, (GROUP + 1) * HEAD_DIM :],
            preferred_element_type=jnp.float32,
        ).astype(jnp.bfloat16)
        for h in range(GROUP):
            out_ref[rows, h * HEAD_DIM : (h + 1) * HEAD_DIM] = mixed[h * block : (h + 1) * block]


def attend_turned(qkv, lens):
    count = qkv.shape[0]
    vmem = pl.BlockSpec(memory_space=pltpu.VMEM)
    return pl.pallas_call(
        attend_kernel,
        out_shape=jax.ShapeDtypeStruct((count, GROUP * HEAD_DIM), jnp.bfloat16),
        in_specs=[pl.BlockSpec(memory_space=pltpu.SMEM), vmem],
        out_specs=vmem,
        compiler_params=pltpu.CompilerParams(vmem_limit_bytes=32 << 20),
        name="attention",
    )(lens, qkv)


def project_kernel(
    cuts, lens_ref, gain_ref, bias_ref, w_hbm, tok_hbm, out_ref,
    wide_w, wb, full, tok, pieces, scale, total, cosine, sine, side, sides,
    tok_sem, w_sem, first_send, first_recv, side_send, side_recv,
    ring_send, ring_recv, trail_send, trail_recv,
):
    req, tp = lax.axis_index("req"), lax.axis_index("tp")
    count, depth = tok.shape
    shard = wb.shape[1]
    width = full.shape[2]
    z, x = req // 2, req % 2
    y, core = tp // 2, tp % 2
    place = (1 - x) * z + x * (7 - z)

    def req_at(pos):
        pos = pos % 8
        far = pos // 4
        return (1 - far) * (2 * pos) + far * (2 * (7 - pos) + 1)

    right, left = req_at(place + 1), req_at(place + 7)
    peers = (2 * y + 1 - core, 2 * (1 - y) + core, 2 * (1 - y) + 1 - core)
    own = 4 * req + tp

    barrier = pltpu.get_barrier_semaphore()
    for peer in peers:
        pl.semaphore_signal(barrier, inc=1, device_id=(req, peer), device_id_type=MESH)
    for near in (left, right):
        pl.semaphore_signal(barrier, inc=1, device_id=(near, tp), device_id_type=MESH)

    loads = []
    for k, t in enumerate(peers + (tp,)):
        copy = pltpu.make_async_copy(
            w_hbm.at[:, pl.ds(pl.multiple_of(t * width, 128), width)], wide_w.at[k], w_sem.at[k]
        )
        loads.append(copy)
    for k in (0, 3, 1, 2):
        loads[k].start()
    tok_copy = pltpu.make_async_copy(tok_hbm, tok, tok_sem)
    tok_copy.start()

    def rounded(v):
        return v.astype(jnp.bfloat16).astype(jnp.float32)

    side[...] = jnp.zeros_like(side)
    side[0:1, 0:shard] = rounded(gain_ref[...])
    side[1:2, :] = rounded(bias_ref[:, 0:128])
    side[2:3, 0 : width // 8 - 128] = rounded(bias_ref[:, 128:])

    pl.semaphore_wait(barrier, 5)
    side_firsts = []
    for k, peer in enumerate(peers):
        copy = pltpu.make_async_remote_copy(
            src_ref=side, dst_ref=sides.at[core, req, y],
            send_sem=side_send.at[k], recv_sem=side_recv.at[k],
            device_id=(req, peer), device_id_type=MESH,
        )
        copy.start()
        side_firsts.append(copy)
    sides[core, req, y] = side[...]
    firsts = {}
    for k in (0, 3, 1, 2):
        loads[k].wait()
        if k == 3:
            full[own, 0:shard, :] = wide_w[k].astype(jnp.bfloat16)
            continue
        wb[k] = wide_w[k].astype(jnp.bfloat16)
        copy = pltpu.make_async_remote_copy(
            src_ref=wb.at[k], dst_ref=full.at[own, pl.ds(0, shard)],
            send_sem=first_send.at[k], recv_sem=first_recv.at[k],
            device_id=(req, peers[k]), device_id_type=MESH,
        )
        copy.start()
        firsts[k] = copy

    ring = {}
    trail = {}

    def source_of(way, hop):
        return req_at(place + 8 - hop) if way == 0 else req_at(place + hop)

    def slot_of(way, hop, piece):
        row = y if piece == 0 else 1 - y
        return 4 * source_of(way, hop) + 2 * row + way

    def send(way, hop, piece, part):
        rows = full.at[slot_of(way, hop, piece), pl.ds(cuts[part], cuts[part + 1] - cuts[part])]
        copy = pltpu.make_async_remote_copy(
            src_ref=rows, dst_ref=rows,
            send_sem=ring_send.at[way, hop, piece, part],
            recv_sem=ring_recv.at[way, hop, piece, part],
            device_id=(right if way == 0 else left, tp), device_id_type=MESH,
        )
        copy.start()
        ring[way, hop, piece, part] = copy

    def send_trail(way, hop):
        block = sides.at[way, source_of(way, hop)]
        copy = pltpu.make_async_remote_copy(
            src_ref=block, dst_ref=block,
            send_sem=trail_send.at[way, hop], recv_sem=trail_recv.at[way, hop],
            device_id=(right if way == 0 else left, tp), device_id_type=MESH,
        )
        copy.start()
        trail[way, hop] = copy

    def place_pieces(quarter):
        group = depth // 4
        base = quarter * group

        @pl.loop(0, count // 64)
        def _(i):
            rows = pl.ds(pl.multiple_of(i * 64, 64), 64)
            for k in range(8):
                lo = base + shard * k
                at = lo // 128 * 128
                span = tok[rows, at : min(at + 256, depth)].astype(jnp.float32)
                size = span.shape[1]
                if lo > at:
                    span = pltpu.roll(span, size - (lo - at), 1)
                lane = lax.broadcasted_iota(jnp.int32, (64, 128), 1)
                part = jnp.where(lane < shard, span[:, 0:128], 0.0)
                pieces[8 * quarter + k, rows, :] = part.astype(jnp.bfloat16)

    def factor(slot, way):
        gain = sides[way, slot // 4, slot % 4 // 2, 0:1, :]
        return (pieces[slot].astype(jnp.float32) * scale[...] * gain).astype(jnp.bfloat16)

    def factors(hop, piece):
        return jnp.concatenate(
            [factor(slot_of(way, hop, piece), way) for way in range(2)], axis=1
        )

    def blocks(hop, piece, columns):
        return jnp.concatenate(
            [full[slot_of(way, hop, piece), :, columns] for way in range(2)], axis=0
        )

    def multiply(hop, piece, begin=False):
        lhs = factors(hop, piece)
        for n in range(3):
            part = slice(n * (width // 3), (n + 1) * (width // 3))
            product = jnp.dot(lhs, blocks(hop, piece, part), preferred_element_type=jnp.float32)
            if begin:
                total[:, part] = product
            else:
                total[:, part] += product

    due = {
        3: ((0, 1),),
        4: ((1, 0), (2, 0), (1, 1)),
        5: ((3, 0), (2, 1), (4, 0)),
        6: ((5, 0), (3, 1), (4, 1), (6, 0)),
        7: ((5, 1), (7, 0), (6, 1)),
    }
    parts = len(cuts) - 1
    for step in range(8):
        if step == 0:
            firsts[0].wait_recv()
        for part in range(parts):
            for way in range(2):
                if step >= 1:
                    ring[way, step - 1, 0, part].wait_recv()
                if step <= 6:
                    send(way, step, 0, part)
        if step == 0:
            for copy in side_firsts:
                copy.wait_recv()
        for way in range(2):
            if step >= 1:
                trail[way, step - 1].wait_recv()
            if step <= 6:
                send_trail(way, step)
        if step == 1:
            firsts[1].wait_recv()
            firsts[2].wait_recv()
        if step >= 1:
            for part in range(parts):
                for way in range(2):
                    if step >= 2:
                        ring[way, step - 2, 1, part].wait_recv()
                    send(way, step - 1, 1, part)
        if step == 0:
            @pl.loop(0, full.shape[0])
            def _(i):
                full[i, shard:, :] = jnp.zeros((full.shape[1] - shard, width), jnp.bfloat16)

            tok_copy.wait()

            @pl.loop(0, count // 32)
            def _(i):
                rows = pl.ds(pl.multiple_of(i * 32, 32), 32)
                wide = tok[rows, :].astype(jnp.float32)
                mean = jnp.sum(wide * wide, axis=-1, keepdims=True) * (1.0 / depth)
                scale[rows, :] = jnp.broadcast_to(lax.rsqrt(mean + 1e-06), (32, 128))
        elif step == 1:
            place_pieces(0)
            place_pieces(1)
        elif step == 2:
            place_pieces(2)
            place_pieces(3)
        elif step == 3:
            at = lax.broadcasted_iota(jnp.int32, (count, 1), 0)
            pos = (at - start_of(at, lens_ref)).astype(jnp.float32)
            lane = lax.broadcasted_iota(jnp.int32, (1, HEAD_DIM), 1)
            half = HEAD_DIM // 2
            freqs = jnp.exp(
                -((lane % half).astype(jnp.float32) * 2.0 / HEAD_DIM) * math.log(1000000.0)
            )
            angle = pos * freqs
            cosine[...] = jnp.cos(angle)
            sine[...] = jnp.where(lane < half, -1.0, 1.0) * jnp.sin(angle)
            multiply(0, 0, True)
        for distance, piece in due.get(step, ()):
            multiply(distance, piece)
    lines = [
        sides[(8 * tp + i) % 2, (8 * tp + i) // 4, (8 * tp + i) % 4 // 2] for i in range(8)
    ]
    bias = jnp.zeros((8, width), jnp.float32)
    for i, both in enumerate(lines):
        line = jnp.concatenate(
            [
                pltpu.roll(both, 7, 0), pltpu.roll(both, 6, 0),
                jnp.zeros((8, width - 256), jnp.float32),
            ],
            axis=1,
        )
        bias = bias + (pltpu.roll(line, width // 8 * i, 1) if i else line)
    bias = bias[0:1, :]
    lhs = factors(7, 1)
    for part in range(parts):
        for way in range(2):
            ring[way, 6, 1, part].wait_recv()
    for n in range(3):
        lo = n * (width // 3)
        part = slice(lo, lo + width // 3)
        product = jnp.dot(lhs, blocks(7, 1, part), preferred_element_type=jnp.float32)
        joined = total[:, part] + product + bias[:, part]
        for k in range(3):
            head = 3 * n + k
            v = joined[:, k * HEAD_DIM : (k + 1) * HEAD_DIM]
            out_ref[:, head * HEAD_DIM : (head + 1) * HEAD_DIM] = (
                rotated(v, cosine[...], sine[...]) if head <= GROUP else v.astype(jnp.bfloat16)
            )
    for copy in (
        list(firsts.values()) + side_firsts + list(ring.values()) + list(trail.values())
    ):
        copy.wait_send()


def project(tokens, norm_gain, qkv_weight, qkv_bias, lens):
    count, depth = tokens.shape
    shard, columns = qkv_weight.shape
    width = columns // 4
    half = shard // 32 * 16
    cuts = (0, shard - half, shard)
    parts = len(cuts) - 1
    vmem = pl.BlockSpec(memory_space=pltpu.VMEM)
    hbm = pl.BlockSpec(memory_space=pl.ANY)
    dma = pltpu.SemaphoreType.DMA
    f32, bf16 = jnp.float32, jnp.bfloat16
    return pl.pallas_call(
        functools.partial(project_kernel, cuts),
        out_shape=jax.ShapeDtypeStruct((count, width), bf16),
        in_specs=[pl.BlockSpec(memory_space=pltpu.SMEM), vmem, vmem, hbm, hbm],
        out_specs=vmem,
        scratch_shapes=[
            pltpu.VMEM((4, shard, width), f32),
            pltpu.VMEM((3, shard, width), bf16),
            pltpu.VMEM((32, 128, width), bf16),
            pltpu.VMEM((count, depth), bf16),
            pltpu.VMEM((32, count, 128), bf16),
            pltpu.VMEM((count, 128), f32),
            pltpu.VMEM((count, width), f32),
            pltpu.VMEM((count, HEAD_DIM), f32),
            pltpu.VMEM((count, HEAD_DIM), f32),
            pltpu.VMEM((8, 128), f32),
            pltpu.VMEM((2, 8, 2, 8, 128), f32),
            dma, dma((4,)),
            dma((3,)), dma((3,)), dma((3,)), dma((3,)),
            dma((2, 7, 2, parts)), dma((2, 7, 2, parts)), dma((2, 7)), dma((2, 7)),
        ],
        compiler_params=pltpu.CompilerParams(
            collective_id=0, has_side_effects=True, vmem_limit_bytes=52 << 20
        ),
        name="project",
    )(lens, norm_gain.reshape(1, shard), qkv_bias.reshape(1, -1), qkv_weight, tokens)


def turn_plain(joined, lens):
    count = joined.shape[0]
    half = HEAD_DIM // 2
    pos = jnp.arange(count, dtype=jnp.int32) - starts(lens, count)
    freqs = jnp.exp(-(jnp.arange(half, dtype=jnp.float32) * 2.0 / HEAD_DIM) * math.log(1000000.0))
    angle = pos.astype(jnp.float32)[:, None] * freqs[None, :]
    cosine = jnp.tile(jnp.cos(angle), (1, 2))[:, None, :]
    sine = jnp.tile(jnp.sin(angle), (1, 2))[:, None, :]
    heads = joined.reshape(count, GROUP + 2, HEAD_DIM)
    spun = jnp.concatenate([-heads[..., half:], heads[..., :half]], axis=-1)
    turned = (heads * cosine + spun * sine)[:, : GROUP + 1]
    both = jnp.concatenate([turned, heads[:, GROUP + 1 :]], axis=1)
    return both.reshape(count, -1).astype(jnp.bfloat16)


def project_plain(tokens, norm_gain, qkv_weight, qkv_bias):
    tp_count = lax.axis_size("tp")
    req_count = lax.axis_size("req")
    tp_place = lax.axis_index("tp")
    gain_full, bias_full = (
        lax.all_gather(norm_gain.astype(jnp.bfloat16), ("req", "tp"), axis=0, tiled=True),
        lax.all_gather(qkv_bias.astype(jnp.bfloat16), ("req", "tp"), axis=0, tiled=True),
    )
    width = bias_full.shape[0] // tp_count
    bias_block = lax.dynamic_slice_in_dim(bias_full, tp_place * width, width).astype(jnp.float32)
    normed = normalize(tokens, gain_full)
    weight_b = qkv_weight.astype(jnp.bfloat16)
    count = tokens.shape[0]
    gathered = lax.all_gather(weight_b, "req", axis=0, tiled=True)
    regrouped = lax.all_to_all(gathered, "tp", split_axis=1, concat_axis=0, tiled=True)
    shard_rows = weight_b.shape[0]
    reordered = (
        normed.reshape(count, req_count, tp_count, shard_rows)
        .transpose(0, 2, 1, 3)
        .reshape(count, -1)
    )
    joined = jnp.dot(reordered, regrouped, preferred_element_type=jnp.float32)
    return joined + bias_block[None, :]


def shards(small, tokens, norm_gain, qkv_weight, qkv_bias, lengths):
    if small:
        qkv = project(tokens, norm_gain, qkv_weight, qkv_bias, lengths)
    else:
        qkv = turn_plain(project_plain(tokens, norm_gain, qkv_weight, qkv_bias), lengths[0])
    return attend_turned(qkv, lengths)


def solution(mesh):
    placed = (
        P("req", None),
        P(("req", "tp")),
        P(("req", "tp"), None),
        P(("req", "tp")),
        P("req", None),
    )
    small = mesh.shape["req"] == 8 and mesh.shape["tp"] == 4
    return jax.shard_map(
        functools.partial(shards, small),
        mesh=mesh, in_specs=placed, out_specs=P("req", "tp"), check_vma=False,
    )
```

time: 332 us -> 95.6 us (0.29)
  waiting for transfers between devices: 126 us -> 0 us
  blocking collectives: 123 us -> 0 us
  Pallas kernels: 0 us -> 93.5 us
  local copies, waits for them, and re-layouts: 34.9 us -> 1.99 us
  matrix products: 15.2 us -> 0 us
  between operations: 13.6 us -> 0.01 us
  other arithmetic: 12.6 us -> 0 us
  starting transfers between devices: 5.76 us -> 0 us
    all_gather x1 -> x0, waiting for transfers between devices: 126 us -> none  [shards(): gathered = lax.all_gather(weight_b, 'req', axis=0, tiled=True)]
    unnamed x1 -> x0, blocking collectives: 123 us -> none
    pallas_call x0 -> x2, Pallas kernels: none -> 93.5 us  [the longest x1 89.1 us: project(): pl.pallas_call(functools.partial(project_kernel, cuts), out_shape=jax.Sha...]
    dot_general x3 -> x0, matrix products: 15.2 us -> none  [the longest x1 10.8 us: shards(): joined = jnp.dot(reordered, regrouped, preferred_element_type=jnp.float32)]
    all_to_all x1 -> x0, local copies, waits for them, and re-layouts: 11.5 us -> none  [shards(): lax.all_to_all(gathered, 'tp', split_axis=1, concat_axis=0, tiled=True)]
    all_gather x1 -> x0, local copies, waits for them, and re-layouts: 11.4 us -> none  [shards(): gathered = lax.all_gather(weight_b, 'req', axis=0, tiled=True)]
    convert_element_type x6 -> x0, other arithmetic: 5.9 us -> none  [the longest x1 3.09 us: normalize(): (wide * lax.rsqrt(meansq + 1e-06) * gain.astype(jnp.float32)).astype(jnp....]
    all_to_all x1 -> x0, starting transfers between devices: 5.76 us -> none  [shards(): lax.all_to_all(gathered, 'tp', split_axis=1, concat_axis=0, tiled=True)]
  transfers between devices with their start and end apart: 2 -> 0, of which waited for: 1 -> 0; matrix products, arithmetic and copies ran while one was open for 5% -> 0% of each run, Pallas kernels for 0% -> 0%
where the time goes in v2:
time: 95.6 us; the launch traced here: 95.5 us
  Pallas kernels  93.5 us (98%)
  local copies, waits for them, and re-layouts  1.99 us (2%)
    pallas_call x1, Pallas kernels, project(): pl.pallas_call(functools.partial(project_kernel, cuts), out_shape=jax.Sha...  89.1 us
    pallas_call x1, Pallas kernels, attend_turned(): pl.pallas_call(attend_kernel, out_shape=jax.ShapeDtypeStruct((count, GROU...  4.41 us
    unnamed x6, local copies, waits for them, and re-layouts  1.99 us

profile of v2, /device:TPU:0, one launch (start us, length us, event | category | flops | bytes accessed | tf_op | source)
XLA Modules:
  0.0 95.5 jit_solution(5261673277895285286)
XLA Ops:
  0.0 0.0 copy-start
  0.0 0.7 copy-done
  0.7 0.0 copy-start.1
  0.7 0.7 copy-done.1
  1.3 0.0 copy-start.2
  1.3 0.7 copy-done.2
  2.0 89.1 %project.1.qkv_ref = bf16[512,1152]{1,0:T(8,128)(2,1)S(1)} custom-call(s32[1,4]{1,0:T(1,128)S(1)} %copy-done, f32[1,112]{1,0:T(1,128)S(1)} %bitcast.3, f32[1,144]{1,0:T(1,128)S(1)} %bitcast.2, f32[112,4608]{1,0:T(8,128)} %w_hbm.1, bf16[512,3584]{1,0:T(8,128)(2,1)} %tok_hbm.1), custom_call_target="tpu_custom_call" | custom-call | tf_op jit(solution)/shard_map/project/pallas_call | solution.py:354
  91.1 4.4 %attention.1 = bf16[512,896]{1,0:T(8,128)(2,1)} custom-call(s32[1,4]{1,0:T(1,128)S(1)} %copy-done, bf16[512,1152]{1,0:T(8,128)(2,1)S(1)} %project.1.qkv_ref), custom_call_target="tpu_custom_call" | custom-call | tf_op jit(solution)/shard_map/attention/pallas_call | solution.py:84
Async XLA Ops:
  0.0 0.7 copy-start
  0.7 0.7 copy-start.1
  1.3 0.7 copy-start.2

commit v3 on v2

--- a/solution.py
+++ b/solution.py
@@ -40,60 +40,70 @@
     return start
 
 
-def attend_kernel(lens_ref, qkv_ref, out_ref):
-    count = qkv_ref.shape[0]
+def attend_block(at, query, keys, values, lens_ref):
     block = 128
-    back = -(-(MOST - 1) // block)
-    for at in range(count // block):
-        first = max(0, at - back)
-        wide = (at + 1 - first) * block
-        rows = slice(at * block, (at + 1) * block)
-        seen = slice(first * block, (at + 1) * block)
-        query_at = at * block + lax.broadcasted_iota(jnp.int32, (block, 1), 0)
-        key_at = first * block + lax.broadcasted_iota(jnp.int32, (block, wide), 1)
-        start = start_of(query_at, lens_ref)
-        low = jnp.maximum(query_at - (WINDOW - 1), start)
-        allowed = jnp.logical_and(
-            key_at <= query_at,
-            jnp.logical_or(
-                key_at >= low, jnp.logical_and(key_at >= start, key_at < start + SINKS)
-            ),
-        )
-        query = jnp.concatenate(
-            [qkv_ref[rows, h * HEAD_DIM : (h + 1) * HEAD_DIM] for h in range(GROUP)], axis=0
-        )
-        scores = lax.dot_general(
-            query, qkv_ref[seen, GROUP * HEAD_DIM : (GROUP + 1) * HEAD_DIM],
-            (((1,), (1,)), ((), ())), preferred_element_type=jnp.float32,
-        ) * (1.0 / math.sqrt(HEAD_DIM))
-        scores = jnp.where(allowed[None], scores.reshape(GROUP, block, wide), -1e30)
-        peak = jnp.max(scores, axis=-1, keepdims=True)
-        expo = jnp.exp(scores - peak)
-        weights = (expo * (1.0 / jnp.sum(expo, axis=-1, keepdims=True))).astype(jnp.bfloat16)
-        mixed = jnp.dot(
-            weights.reshape(GROUP * block, wide), qkv_ref[seen, (GROUP + 1) * HEAD_DIM :],
-            preferred_element_type=jnp.float32,
-        ).astype(jnp.bfloat16)
-        for h in range(GROUP):
-            out_ref[rows, h * HEAD_DIM : (h + 1) * HEAD_DIM] = mixed[h * block : (h + 1) * block]
-
-
-def attend_turned(qkv, lens):
+    first = max(0, at - -(-(MOST - 1) // block))
+    wide = (at + 1 - first) * block
+    heads = query.shape[0] // block
+    query_at = at * block + lax.broadcasted_iota(jnp.int32, (block, 1), 0)
+    key_at = first * block + lax.broadcasted_iota(jnp.int32, (block, wide), 1)
+    start = start_of(query_at, lens_ref)
+    low = jnp.maximum(query_at - (WINDOW - 1), start)
+    allowed = jnp.logical_and(
+        key_at <= query_at,
+        jnp.logical_or(key_at >= low, jnp.logical_and(key_at >= start, key_at < start + SINKS)),
+    )
+    seen = slice(first * block, (at + 1) * block)
+    scores = lax.dot_general(
+        query, keys(seen), (((1,), (1,)), ((), ())), preferred_element_type=jnp.float32
+    ) * (1.0 / math.sqrt(HEAD_DIM))
+    scores = jnp.where(allowed[None], scores.reshape(heads, block, wide), -1e30)
+    peak = jnp.max(scores, axis=-1, keepdims=True)
+    expo = jnp.exp(scores - peak)
+    weights = (expo * (1.0 / jnp.sum(expo, axis=-1, keepdims=True))).astype(jnp.bfloat16)
+    return jnp.dot(
+        weights.reshape(heads * block, wide), values(seen), preferred_element_type=jnp.float32
+    ).astype(jnp.bfloat16)
+
+
+def attend_heads(at, heads, shift, source, key, value, out_ref, lens_ref):
+    rows = slice(at * 128, (at + 1) * 128)
+    query = jnp.concatenate(
+        [source[rows, h * HEAD_DIM : (h + 1) * HEAD_DIM] for h in heads], axis=0
+    )
+    mixed = attend_block(at, query, key, value, lens_ref)
+    for i, h in enumerate(heads):
+        column = (h - shift) * HEAD_DIM
+        out_ref[rows, column : column + HEAD_DIM] = mixed[i * 128 : (i + 1) * 128]
+
+
+def attend_kernel(heads, lens_ref, qkv_ref, *refs):
+    out_ref = refs[-1]
+    part = lambda c: lambda seen: qkv_ref[seen, c * HEAD_DIM : (c + 1) * HEAD_DIM]
+    for at in range(qkv_ref.shape[0] // 128):
+        attend_heads(
+            at, range(heads), 0, qkv_ref, part(heads), part(heads + 1), out_ref, lens_ref
+        )
+    if len(refs) > 1:
+        out_ref[:, heads * HEAD_DIM :] = refs[0][...]
+
+
+def attend_turned(lens, qkv, *done):
     count = qkv.shape[0]
     vmem = pl.BlockSpec(memory_space=pltpu.VMEM)
     return pl.pallas_call(
-        attend_kernel,
+        functools.partial(attend_kernel, qkv.shape[1] // HEAD_DIM - 2),
         out_shape=jax.ShapeDtypeStruct((count, GROUP * HEAD_DIM), jnp.bfloat16),
-        in_specs=[pl.BlockSpec(memory_space=pltpu.SMEM), vmem],
+        in_specs=[pl.BlockSpec(memory_space=pltpu.SMEM)] + [vmem] * (1 + len(done)),
         out_specs=vmem,
         compiler_params=pltpu.CompilerParams(vmem_limit_bytes=32 << 20),
         name="attention",
-    )(lens, qkv)
+    )(lens, qkv, *done)
 
 
 def project_kernel(
-    cuts, lens_ref, gain_ref, bias_ref, w_hbm, tok_hbm, out_ref,
-    wide_w, wb, full, tok, pieces, scale, total, cosine, sine, side, sides,
+    lens_hbm, gain_hbm, bias_hbm, w_hbm, tok_hbm, out_ref, done_ref,
+    lens_ref, gain_ref, bias_ref, small_sem, turned, line_ref, wide_w, wb, full, tok, pieces, scale, total, cosine, sine, side, sides,
     tok_sem, w_sem, first_send, first_recv, side_send, side_recv,
     ring_send, ring_recv, trail_send, trail_recv,
 ):
@@ -120,6 +130,14 @@
     for near in (left, right):
         pl.semaphore_signal(barrier, inc=1, device_id=(near, tp), device_id_type=MESH)
 
+    smalls = [
+        pltpu.make_async_copy(source, to, small_sem.at[k])
+        for k, (source, to) in enumerate(
+            ((gain_hbm, gain_ref), (bias_hbm, bias_ref), (lens_hbm, lens_ref))
+        )
+    ]
+    for copy in smalls:
+        copy.start()
     loads = []
     for k, t in enumerate(peers + (tp,)):
         copy = pltpu.make_async_copy(
@@ -134,6 +152,8 @@
     def rounded(v):
         return v.astype(jnp.bfloat16).astype(jnp.float32)
 
+    for copy in smalls:
+        copy.wait()
     side[...] = jnp.zeros_like(side)
     side[0:1, 0:shard] = rounded(gain_ref[...])
     side[1:2, :] = rounded(bias_ref[:, 0:128])
@@ -175,16 +195,31 @@
         row = y if piece == 0 else 1 - y
         return 4 * source_of(way, hop) + 2 * row + way
 
-    def send(way, hop, piece, part):
-        rows = full.at[slot_of(way, hop, piece), pl.ds(cuts[part], cuts[part + 1] - cuts[part])]
+    phases = ((5, 9), (2, 5), (0, 2))
+
+    def send(way, turn, piece):
+        lo, hi = phases[turn // 7]
+        block = full.at[
+            slot_of(way, turn % 7, piece),
+            pl.ds(0, shard),
+            pl.ds(lo * HEAD_DIM, (hi - lo) * HEAD_DIM),
+        ]
         copy = pltpu.make_async_remote_copy(
-            src_ref=rows, dst_ref=rows,
-            send_sem=ring_send.at[way, hop, piece, part],
-            recv_sem=ring_recv.at[way, hop, piece, part],
+            src_ref=block, dst_ref=block,
+            send_sem=ring_send.at[way, turn, piece], recv_sem=ring_recv.at[way, turn, piece],
             device_id=(right if way == 0 else left, tp), device_id_type=MESH,
         )
         copy.start()
-        ring[way, hop, piece, part] = copy
+        ring[way, turn, piece] = copy
+
+    def pass_on(turn, piece):
+        for way in range(2):
+            if turn <= 20 and turn % 7 == 0:
+                send(way, turn, piece)
+            if turn >= 1:
+                ring[way, turn - 1, piece].wait_recv()
+            if turn <= 20 and turn % 7:
+                send(way, turn, piece)
 
     def send_trail(way, hop):
         block = sides.at[way, source_of(way, hop)]
@@ -223,55 +258,80 @@
             [factor(slot_of(way, hop, piece), way) for way in range(2)], axis=1
         )
 
-    def blocks(hop, piece, columns):
-        return jnp.concatenate(
-            [full[slot_of(way, hop, piece), :, columns] for way in range(2)], axis=0
-        )
-
-    def multiply(hop, piece, begin=False):
-        lhs = factors(hop, piece)
-        for n in range(3):
-            part = slice(n * (width // 3), (n + 1) * (width // 3))
-            product = jnp.dot(lhs, blocks(hop, piece, part), preferred_element_type=jnp.float32)
-            if begin:
-                total[:, part] = product
-            else:
-                total[:, part] += product
-
-    due = {
-        3: ((0, 1),),
-        4: ((1, 0), (2, 0), (1, 1)),
-        5: ((3, 0), (2, 1), (4, 0)),
-        6: ((5, 0), (3, 1), (4, 1), (6, 0)),
-        7: ((5, 1), (7, 0), (6, 1)),
-    }
-    parts = len(cuts) - 1
-    for step in range(8):
+    def product(lhs, phase, distance, piece):
+        lo, hi = phases[phase]
+        columns = slice(lo * HEAD_DIM, hi * HEAD_DIM)
+        rhs = jnp.concatenate(
+            [full[slot_of(way, distance, piece), :, columns] for way in range(2)], axis=0
+        )
+        return columns, jnp.dot(lhs, rhs, preferred_element_type=jnp.float32)
+
+    def multiply(phase, distance, piece):
+        columns, term = product(factors(distance, piece), phase, distance, piece)
+        if distance == 0 and piece == 0:
+            total[:, columns] = term
+        else:
+            total[:, columns] += term
+
+    def turn_head(head, joined):
+        column = slice(head * HEAD_DIM, (head + 1) * HEAD_DIM)
+        v = joined + line_ref[0:1, column]
+        return rotated(v, cosine[...], sine[...]) if head <= GROUP else v.astype(jnp.bfloat16)
+
+    def finish(phase):
+        for head in range(*phases[phase]):
+            column = slice(head * HEAD_DIM, (head + 1) * HEAD_DIM)
+            turned[:, column] = turn_head(head, total[:, column])
+
+    def part_of(c):
+        return lambda seen: turned[seen, c * HEAD_DIM : (c + 1) * HEAD_DIM]
+
+    def heads_of(at, heads):
+        attend_heads(
+            at, heads, 2, turned, part_of(GROUP), part_of(GROUP + 1), done_ref, lens_ref
+        )
+
+    def make_bias():
+        bias = jnp.zeros((8, width), jnp.float32)
+        for i in range(8):
+            owner = 8 * tp + i
+            both = sides[owner % 2, owner // 4, owner % 4 // 2]
+            line = jnp.concatenate(
+                [
+                    pltpu.roll(both, 7, 0), pltpu.roll(both, 6, 0),
+                    jnp.zeros((8, width - 256), jnp.float32),
+                ],
+                axis=1,
+            )
+            bias = bias + (pltpu.roll(line, width // 8 * i, 1) if i else line)
+        line_ref[...] = bias
+
+    due = {step: [] for step in range(22)}
+    for d in range(8):
+        for piece in range(2):
+            due[max(6 + d // 3, d + piece)].append((0, d, piece))
+            due[max(9 + d * 3 // 4, 7 + d + piece)].append((1, d, piece))
+            if (d, piece) != (7, 1):
+                due[max(16, 14 + d + piece)].append((2, d, piece))
+
+    for step in range(22):
         if step == 0:
             firsts[0].wait_recv()
-        for part in range(parts):
-            for way in range(2):
-                if step >= 1:
-                    ring[way, step - 1, 0, part].wait_recv()
-                if step <= 6:
-                    send(way, step, 0, part)
+        pass_on(step, 0)
         if step == 0:
             for copy in side_firsts:
                 copy.wait_recv()
-        for way in range(2):
-            if step >= 1:
-                trail[way, step - 1].wait_recv()
-            if step <= 6:
-                send_trail(way, step)
+        if step <= 7:
+            for way in range(2):
+                if step >= 1:
+                    trail[way, step - 1].wait_recv()
+                if step <= 6:
+                    send_trail(way, step)
         if step == 1:
             firsts[1].wait_recv()
             firsts[2].wait_recv()
         if step >= 1:
-            for part in range(parts):
-                for way in range(2):
-                    if step >= 2:
-                        ring[way, step - 2, 1, part].wait_recv()
-                    send(way, step - 1, 1, part)
+            pass_on(step - 1, 1)
         if step == 0:
             @pl.loop(0, full.shape[0])
             def _(i):
@@ -285,13 +345,9 @@
                 wide = tok[rows, :].astype(jnp.float32)
                 mean = jnp.sum(wide * wide, axis=-1, keepdims=True) * (1.0 / depth)
                 scale[rows, :] = jnp.broadcast_to(lax.rsqrt(mean + 1e-06), (32, 128))
-        elif step == 1:
-            place_pieces(0)
-            place_pieces(1)
-        elif step == 2:
-            place_pieces(2)
-            place_pieces(3)
-        elif step == 3:
+        elif step <= 4:
+            place_pieces(step - 1)
+        elif step == 5:
             at = lax.broadcasted_iota(jnp.int32, (count, 1), 0)
             pos = (at - start_of(at, lens_ref)).astype(jnp.float32)
             lane = lax.broadcasted_iota(jnp.int32, (1, HEAD_DIM), 1)
@@ -302,38 +358,26 @@
             angle = pos * freqs
             cosine[...] = jnp.cos(angle)
             sine[...] = jnp.where(lane < half, -1.0, 1.0) * jnp.sin(angle)
-            multiply(0, 0, True)
-        for distance, piece in due.get(step, ()):
-            multiply(distance, piece)
-    lines = [
-        sides[(8 * tp + i) % 2, (8 * tp + i) // 4, (8 * tp + i) % 4 // 2] for i in range(8)
-    ]
-    bias = jnp.zeros((8, width), jnp.float32)
-    for i, both in enumerate(lines):
-        line = jnp.concatenate(
-            [
-                pltpu.roll(both, 7, 0), pltpu.roll(both, 6, 0),
-                jnp.zeros((8, width - 256), jnp.float32),
-            ],
-            axis=1,
-        )
-        bias = bias + (pltpu.roll(line, width // 8 * i, 1) if i else line)
-    bias = bias[0:1, :]
+        for item in due[step]:
+            multiply(*item)
+        if step == 8:
+            make_bias()
+            finish(0)
+        if 9 <= step <= 12:
+            heads_of(step - 9, (5, 6))
+        if step == 15:
+            finish(1)
+        if 16 <= step <= 19:
+            heads_of(step - 16, (2, 3, 4))
+    out_ref[:, 2 * HEAD_DIM :] = turned[:, GROUP * HEAD_DIM :]
     lhs = factors(7, 1)
-    for part in range(parts):
-        for way in range(2):
-            ring[way, 6, 1, part].wait_recv()
-    for n in range(3):
-        lo = n * (width // 3)
-        part = slice(lo, lo + width // 3)
-        product = jnp.dot(lhs, blocks(7, 1, part), preferred_element_type=jnp.float32)
-        joined = total[:, part] + product + bias[:, part]
-        for k in range(3):
-            head = 3 * n + k
-            v = joined[:, k * HEAD_DIM : (k + 1) * HEAD_DIM]
-            out_ref[:, head * HEAD_DIM : (head + 1) * HEAD_DIM] = (
-                rotated(v, cosine[...], sine[...]) if head <= GROUP else v.astype(jnp.bfloat16)
-            )
+    for way in range(2):
+        ring[way, 20, 1].wait_recv()
+    columns, term = product(lhs, 2, 7, 1)
+    joined = total[:, columns] + term
+    for head in range(2):
+        column = slice(head * HEAD_DIM, (head + 1) * HEAD_DIM)
+        out_ref[:, column] = turn_head(head, joined[:, column])
     for copy in (
         list(firsts.values()) + side_firsts + list(ring.values()) + list(trail.values())
     ):
@@ -344,19 +388,25 @@
     count, depth = tokens.shape
     shard, columns = qkv_weight.shape
     width = columns // 4
-    half = shard // 32 * 16
-    cuts = (0, shard - half, shard)
-    parts = len(cuts) - 1
     vmem = pl.BlockSpec(memory_space=pltpu.VMEM)
-    hbm = pl.BlockSpec(memory_space=pl.ANY)
+    hbm = pl.BlockSpec(memory_space=pltpu.HBM)
     dma = pltpu.SemaphoreType.DMA
     f32, bf16 = jnp.float32, jnp.bfloat16
     return pl.pallas_call(
-        functools.partial(project_kernel, cuts),
-        out_shape=jax.ShapeDtypeStruct((count, width), bf16),
-        in_specs=[pl.BlockSpec(memory_space=pltpu.SMEM), vmem, vmem, hbm, hbm],
-        out_specs=vmem,
+        project_kernel,
+        out_shape=(
+            jax.ShapeDtypeStruct((count, 4 * HEAD_DIM), bf16),
+            jax.ShapeDtypeStruct((count, (GROUP - 2) * HEAD_DIM), bf16),
+        ),
+        in_specs=[hbm] * 5,
+        out_specs=(vmem, vmem),
         scratch_shapes=[
+            pltpu.SMEM(lens.shape, jnp.int32),
+            pltpu.VMEM((1, shard), f32),
+            pltpu.VMEM((1, columns // 32), f32),
+            dma((3,)),
+            pltpu.VMEM((count, width), bf16),
+            pltpu.VMEM((8, width), f32),
             pltpu.VMEM((4, shard, width), f32),
             pltpu.VMEM((3, shard, width), bf16),
             pltpu.VMEM((32, 128, width), bf16),
@@ -370,7 +420,7 @@
             pltpu.VMEM((2, 8, 2, 8, 128), f32),
             dma, dma((4,)),
             dma((3,)), dma((3,)), dma((3,)), dma((3,)),
-            dma((2, 7, 2, parts)), dma((2, 7, 2, parts)), dma((2, 7)), dma((2, 7)),
+            dma((2, 21, 2)), dma((2, 21, 2)), dma((2, 7)), dma((2, 7)),
         ],
         compiler_params=pltpu.CompilerParams(
             collective_id=0, has_side_effects=True, vmem_limit_bytes=52 << 20
@@ -421,10 +471,11 @@
 
 def shards(small, tokens, norm_gain, qkv_weight, qkv_bias, lengths):
     if small:
-        qkv = project(tokens, norm_gain, qkv_weight, qkv_bias, lengths)
-    else:
-        qkv = turn_plain(project_plain(tokens, norm_gain, qkv_weight, qkv_bias), lengths[0])
-    return attend_turned(qkv, lengths)
+        return attend_turned(
+            lengths, *project(tokens, norm_gain, qkv_weight, qkv_bias, lengths)
+        )
+    qkv = turn_plain(project_plain(tokens, norm_gain, qkv_weight, qkv_bias), lengths[0])
+    return attend_turned(lengths, qkv)
 
 
 def solution(mesh):

time: 95.6 us -> 112 us (1.17)
  Pallas kernels: 93.5 us -> 110 us
    pallas_call x2, Pallas kernels: 93.5 us -> 110 us  [the longest x1 106 us: project(): pl.pallas_call(project_kernel, out_shape=(jax.ShapeDtypeStruct((count, 4...]
where the time goes in v3:
time: 112 us
  Pallas kernels  110 us (98%)
  local copies, waits for them, and re-layouts  1.99 us (2%)
    pallas_call x1, Pallas kernels, project(): pl.pallas_call(project_kernel, out_shape=(jax.ShapeDtypeStruct((count, 4...  106 us
    pallas_call x1, Pallas kernels, attend_turned(): pl.pallas_call(functools.partial(attend_kernel, qkv.shape[1] // HEAD_DIM...  3.22 us

profile of v3, /device:TPU:0, one launch (start us, length us, event | category | flops | bytes accessed | tf_op | source)
XLA Modules:
  0.0 111.5 jit_solution(13284232197381185883)
XLA Ops:
  0.0 0.0 copy-start
  0.0 0.7 copy-done
  0.7 0.0 copy-start.1
  0.7 0.7 copy-done.1
  1.3 0.0 copy-start.2
  1.3 0.7 copy-done.2
  2.0 106.3 %project.1 = (bf16[512,512]{1,0:T(8,128)(2,1)S(1)}, bf16[512,640]{1,0:T(8,128)(2,1)S(1)}) custom-call(s32[1,4]{1,0:T(1,128)S(1)} %copy-done, f32[1,112]{1,0:T(1,128)S(1)} %bitcast.3, f32[1,144]{1,0:T(1,128)S(1)} %bitcast.2, f32[112,4608]{1,0:T(8,128)} %w_hbm.1, bf16[512,3584]{1,0:T(8,128)(2,1)} %tok_hbm.1), custom_call_target="tpu_custom_call" | custom-call | tf_op jit(solution)/shard_map/project/pallas_call | solution.py:395
  108.3 3.2 %attention.1 = bf16[512,896]{1,0:T(8,128)(2,1)} custom-call(s32[1,4]{1,0:T(1,128)S(1)} %copy-done, bf16[512,512]{1,0:T(8,128)(2,1)S(1)} %get-tuple-element.7.qkv_ref, bf16[512,640]{1,0:T(8,128)(2,1)S(1)} %get-tuple-element.8.refs_0_), custom_call_target="tpu_custom_call" | custom-call | tf_op jit(solution)/shard_map/attention/pallas_call | solution.py:94
Async XLA Ops:
  0.0 0.7 copy-start
  0.7 0.7 copy-start.1
  1.3 0.7 copy-start.2

commit v4 on v2

--- a/solution.py
+++ b/solution.py
@@ -92,8 +92,8 @@
 
 
 def project_kernel(
-    cuts, lens_ref, gain_ref, bias_ref, w_hbm, tok_hbm, out_ref,
-    wide_w, wb, full, tok, pieces, scale, total, cosine, sine, side, sides,
+    cuts, lens_hbm, gain_hbm, bias_hbm, w_hbm, tok_hbm, out_ref,
+    lens_ref, gain_ref, bias_ref, small_sem, wide_w, wb, full, tok, pieces, scale, total, cosine, sine, side, sides,
     tok_sem, w_sem, first_send, first_recv, side_send, side_recv,
     ring_send, ring_recv, trail_send, trail_recv,
 ):
@@ -120,6 +120,14 @@
     for near in (left, right):
         pl.semaphore_signal(barrier, inc=1, device_id=(near, tp), device_id_type=MESH)
 
+    smalls = [
+        pltpu.make_async_copy(source, to, small_sem.at[k])
+        for k, (source, to) in enumerate(
+            ((gain_hbm, gain_ref), (bias_hbm, bias_ref), (lens_hbm, lens_ref))
+        )
+    ]
+    for copy in smalls:
+        copy.start()
     loads = []
     for k, t in enumerate(peers + (tp,)):
         copy = pltpu.make_async_copy(
@@ -134,6 +142,8 @@
     def rounded(v):
         return v.astype(jnp.bfloat16).astype(jnp.float32)
 
+    for copy in smalls:
+        copy.wait()
     side[...] = jnp.zeros_like(side)
     side[0:1, 0:shard] = rounded(gain_ref[...])
     side[1:2, :] = rounded(bias_ref[:, 0:128])
@@ -348,15 +358,19 @@
     cuts = (0, shard - half, shard)
     parts = len(cuts) - 1
     vmem = pl.BlockSpec(memory_space=pltpu.VMEM)
-    hbm = pl.BlockSpec(memory_space=pl.ANY)
+    hbm = pl.BlockSpec(memory_space=pltpu.HBM)
     dma = pltpu.SemaphoreType.DMA
     f32, bf16 = jnp.float32, jnp.bfloat16
     return pl.pallas_call(
         functools.partial(project_kernel, cuts),
         out_shape=jax.ShapeDtypeStruct((count, width), bf16),
-        in_specs=[pl.BlockSpec(memory_space=pltpu.SMEM), vmem, vmem, hbm, hbm],
+        in_specs=[hbm] * 5,
         out_specs=vmem,
         scratch_shapes=[
+            pltpu.SMEM(lens.shape, jnp.int32),
+            pltpu.VMEM((1, shard), f32),
+            pltpu.VMEM((1, columns // 32), f32),
+            dma((3,)),
             pltpu.VMEM((4, shard, width), f32),
             pltpu.VMEM((3, shard, width), bf16),
             pltpu.VMEM((32, 128, width), bf16),

time: 95.6 us -> 95.1 us (level)
  no operation moved by 1% of the time
where the time goes in v4:
time: 95.1 us; the launch traced here: 94.9 us
  Pallas kernels  92.9 us (98%)
  local copies, waits for them, and re-layouts  1.99 us (2%)
    pallas_call x1, Pallas kernels, project(): pl.pallas_call(functools.partial(project_kernel, cuts), out_shape=jax.Sha...  88.5 us
    pallas_call x1, Pallas kernels, attend_turned(): pl.pallas_call(attend_kernel, out_shape=jax.ShapeDtypeStruct((count, GROU...  4.41 us
    unnamed x6, local copies, waits for them, and re-layouts  1.99 us

profile of v4, /device:TPU:0, one launch (start us, length us, event | category | flops | bytes accessed | tf_op | source)
XLA Modules:
  0.0 94.9 jit_solution(7776236941765396061)
XLA Ops:
  0.0 0.0 copy-start
  0.0 0.7 copy-done
  0.7 0.0 copy-start.1
  0.7 0.7 copy-done.1
  1.3 0.0 copy-start.2
  1.3 0.7 copy-done.2
  2.0 88.5 %project.1.qkv_ref = bf16[512,1152]{1,0:T(8,128)(2,1)S(1)} custom-call(s32[1,4]{1,0:T(1,128)S(1)} %copy-done, f32[1,112]{1,0:T(1,128)S(1)} %bitcast.3, f32[1,144]{1,0:T(1,128)S(1)} %bitcast.2, f32[112,4608]{1,0:T(8,128)} %w_hbm.1, bf16[512,3584]{1,0:T(8,128)(2,1)} %tok_hbm.1), custom_call_target="tpu_custom_call" | custom-call | tf_op jit(solution)/shard_map/project/pallas_call | solution.py:364
  90.5 4.4 %attention.1 = bf16[512,896]{1,0:T(8,128)(2,1)} custom-call(s32[1,4]{1,0:T(1,128)S(1)} %copy-done, bf16[512,1152]{1,0:T(8,128)(2,1)S(1)} %project.1.qkv_ref), custom_call_target="tpu_custom_call" | custom-call | tf_op jit(solution)/shard_map/attention/pallas_call | solution.py:84
Async XLA Ops:
  0.0 0.7 copy-start
  0.7 0.7 copy-start.1
  1.3 0.7 copy-start.2

commit v5 on v4

--- a/solution.py
+++ b/solution.py
@@ -86,7 +86,7 @@
         out_shape=jax.ShapeDtypeStruct((count, GROUP * HEAD_DIM), jnp.bfloat16),
         in_specs=[pl.BlockSpec(memory_space=pltpu.SMEM), vmem],
         out_specs=vmem,
-        compiler_params=pltpu.CompilerParams(vmem_limit_bytes=32 << 20),
+        compiler_params=pltpu.CompilerParams(vmem_limit_bytes=64 << 20),
         name="attention",
     )(lens, qkv)
 
@@ -387,7 +387,7 @@
             dma((2, 7, 2, parts)), dma((2, 7, 2, parts)), dma((2, 7)), dma((2, 7)),
         ],
         compiler_params=pltpu.CompilerParams(
-            collective_id=0, has_side_effects=True, vmem_limit_bytes=52 << 20
+            collective_id=0, has_side_effects=True, vmem_limit_bytes=64 << 20
         ),
         name="project",
     )(lens, norm_gain.reshape(1, shard), qkv_bias.reshape(1, -1), qkv_weight, tokens)

time: 95.1 us -> 94.7 us (level)
  local copies, waits for them, and re-layouts: 1.99 us -> 0 us
  Pallas kernels: 92.9 us -> 94.6 us
    unnamed x6 -> x0, local copies, waits for them, and re-layouts: 1.99 us -> none
where the time goes in v5:
time: 94.7 us; the launch traced here: 94.6 us
  Pallas kernels  94.6 us (100%)
    pallas_call x1, Pallas kernels, project(): pl.pallas_call(functools.partial(project_kernel, cuts), out_shape=jax.Sha...  89.4 us
    pallas_call x1, Pallas kernels, attend_turned(): pl.pallas_call(attend_kernel, out_shape=jax.ShapeDtypeStruct((count, GROU...  5.16 us

profile of v5, /device:TPU:0, one launch (start us, length us, event | category | flops | bytes accessed | tf_op | source)
XLA Modules:
  0.0 94.6 jit_solution(17883604696156734810)
XLA Ops:
  0.0 89.4 %project.1.qkv_ref = bf16[512,1152]{1,0:T(8,128)(2,1)} custom-call(s32[1,4]{1,0:T(1,128)} %lens_ref.1, f32[1,112]{1,0:T(1,128)} %bitcast.3, f32[1,144]{1,0:T(1,128)} %bitcast.2, f32[112,4608]{1,0:T(8,128)} %w_hbm.1, bf16[512,3584]{1,0:T(8,128)(2,1)} %tok_hbm.1), custom_call_target="tpu_custom_call" | custom-call | tf_op jit(solution)/shard_map/project/pallas_call | solution.py:364
  89.4 5.2 %attention.1 = bf16[512,896]{1,0:T(8,128)(2,1)} custom-call(s32[1,4]{1,0:T(1,128)} %lens_ref.1, bf16[512,1152]{1,0:T(8,128)(2,1)} %project.1.qkv_ref), custom_call_target="tpu_custom_call" | custom-call | tf_op jit(solution)/shard_map/attention/pallas_call | solution.py:84
